TPU v7x, 32 devices: a whole 2x2x4 slice. The times are simulated.
32 devices in a mesh: mid: 16 (over z, y, x), fin: 2 (over core).
Axes of the slice: x: 2, y: 2, z: 4, core: 2. Of those that a mesh axis runs over, the one named last changes fastest.
Arguments:
- history: float32 [256, 16, 64, 128], P('mid', 'fin'), may hold values from -6 to 6
- sigma: float32 [4, 256, 64, 128], P(None, 'mid', 'fin'), may hold values from -0.0234375 to 0.0234375
- propagator: float32 [64, 128], replicated, may hold values from -0.375 to 0.375
Outputs:
- new_rows: float32 [4, 16, 64, 128], P(None, 'fin', 'mid')
All inputs are finite; a program needn't handle non-finite values.
Results may differ from a plain program's by a relative error of at most 0.0003.
Values sent between devices are 32-bit elements; how exact they have to be, the bound alone decides.
A program may use at most 128 MiB of HBM per device.

v0:
```python
import jax
import jax.numpy as jnp
from jax import lax
from jax.sharding import PartitionSpec as P

STEPS = 4


def from_root(value, axis, source):
    kept = jnp.where(lax.axis_index(axis) == source, value, 0).astype(value.dtype)
    return lax.psum(kept, axis)


def turn_pair(block, axis):
    half = block.shape[-1] // 2
    turned = jnp.concatenate([-block[..., half:], block[..., :half]], axis=-1)
    return jnp.concatenate([block, turned], axis=axis)


def integral(kernel, block, keep):
    masked = block * keep[:, :, None, None]
    stacked = turn_pair(masked, 2)
    return jnp.einsum("sik,sckj->cij", kernel, stacked, precision=lax.Precision.HIGHEST)


def propagate(weight, latest):
    stacked = turn_pair(latest, 1)
    return jnp.einsum("ik,ckj->cij", weight, stacked, precision=lax.Precision.HIGHEST)


def on_device(history, sigma, propagator):
    mid_count = lax.axis_size("mid")
    fin_count = lax.axis_size("fin")
    mid_index = lax.axis_index("mid")
    fin_index = lax.axis_index("fin")
    local_slots = history.shape[0]
    local_cols = history.shape[1]
    orbitals = history.shape[2]
    width = local_slots * mid_count
    ncol = local_cols * fin_count
    slot_ids = mid_index * local_slots + jnp.arange(local_slots, dtype=jnp.int32)
    col_ids = fin_index * local_cols + jnp.arange(local_cols, dtype=jnp.int32)
    col_times = col_ids * width // ncol
    row_count = orbitals // mid_count
    row_start = mid_index * row_count
    latest = from_root(history[local_slots - 1], "mid", mid_count - 1)
    state = history
    outputs = []
    for step in range(STEPS):
        kernel = lax.all_gather(sigma[step], "fin", axis=1, tiled=True)
        slot_times = jnp.where(slot_ids >= step, slot_ids, slot_ids + width)
        keep = (slot_times[:, None] >= col_times[None, :]).astype(jnp.float32)
        partial_value = integral(kernel, state, keep)
        memory = lax.psum(partial_value, "mid")
        new_row = propagate(propagator, latest) + memory
        row_piece = lax.dynamic_slice_in_dim(new_row, row_start, row_count, 1)
        outputs.append(row_piece)
        owner = (slot_ids == step)[:, None, None, None]
        state = jnp.where(owner, new_row[None], state)
        latest = new_row
    return jnp.stack(outputs)


def solution(mesh):
    in_specs = (P("mid", "fin", None, None), P(None, "mid", "fin", None), P())
    out_specs = P(None, "fin", "mid", None)
    return jax.shard_map(
        on_device, mesh=mesh, in_specs=in_specs, out_specs=out_specs, check_vma=False
    )
```

profile of v0, /device:TPU:0, one launch (start us, length us, event | category | flops | bytes accessed | tf_op | source)
XLA Modules:
  0.0 508.6 jit_solution(6335334844309072589)
XLA Ops:
  6.5 0.0 copy-start
  6.5 0.0 all-reduce.12.cloned.1.call-start
  6.6 0.1 compare_convert_fusion.3
  6.7 2.5 copy_multiply_fusion
  9.2 0.0 copy-start.1
  9.2 0.0 copy-start.2
  9.2 4.6 slice_negate_fusion.3
  13.9 0.0 copy-done.1
  13.9 0.0 copy-done.2
  13.9 0.1 fusion.80
  13.9 2.3 all-gather
  16.2 1.7 select_bitcast_fusion
  17.9 10.1 %fusion.37 = f32[8,64,128]{2,1,0:T(8,128)} fusion(f32[16,8,64,64]{3,2,0,1:T(8,128)} %get-tuple-element.14, f32[16,8,64,64]{3,2,0,1:T(8,128)} %get-tuple-element.13, f32[16,8,64,128]{3,2,0,1:T(8,128)} %copy-done.1, f32[1,16,64,128]{3,2,1,0:T(8,128)S(1)} %all-gather), kind=kOutput, calls=%fused_computation.43 | convolution fusion | flops 1614807040 | bytes 9175040 | tf_op jit(solution)/shard_map/sik,sckj->cij/dot_general | solution.py:23
  28.0 0.0 all-reduce.12.cloned.1.call-update
  28.0 0.0 all-reduce.6.cloned.1.call-start
  28.1 2.2 all-gather.1
  30.3 2.2 all-gather.2
  32.5 2.3 all-gather.3
  34.8 105.2 %all-reduce.12.cloned.1.call-done = (f32[8,64,128]{2,1,0:T(8,128)}, f32[8,64,128]{2,1,0:T(8,128)}) async-done(((f32[8,64,128]{2,1,0:T(8,128)}, f32[8,64,128]{2,1,0:T(8,128)}), (f32[8,64,128]{2,1,0:T(8,128)}, f32[8,64,128]{2,1,0:T(8,128)})) %all-reduce.12.cloned.1.call-update) | async-done | bytes 524304 | tf_op jit(solution)/shard_map/psum | solution.py:54
  140.1 1.2 slice_negate_fusion.7
  141.2 0.0 copy-done
  141.2 1.5 fusion.27
  142.7 2.7 fusion.24
  145.4 1.7 slice_negate_fusion.2
  147.1 6.8 %fusion.34 = f32[8,64,128]{2,1,0:T(8,128)} fusion(f32[16,8,64,64]{3,2,0,1:T(8,128)S(1)} %get-tuple-element.12, f32[16,8,64,64]{3,2,0,1:T(8,128)S(1)} %get-tuple-element.11, f32[16,8,64,128]{3,2,0,1:T(8,128)S(1)} %fusion.24, f32[1,16,64,128]{3,2,1,0:T(8,128)S(1)} %all-gather.1), kind=kOutput, calls=%fused_computation.42 | convolution fusion | flops 1614807040 | bytes 9175040 | tf_op jit(solution)/shard_map/sik,sckj->cij/dot_general | solution.py:23
  153.9 0.0 all-reduce.6.cloned.1.call-update
  153.9 0.3 all-reduce.8.cloned.1.call-start
  154.2 0.1 slice_negate_fusion.6
  154.3 106.5 %all-reduce.6.cloned.1.call-done = f32[8,64,128]{2,1,0:T(8,128)} async-done(((f32[8,64,128]{2,1,0:T(8,128)}), f32[8,64,128]{2,1,0:T(8,128)}) %all-reduce.6.cloned.1.call-update) | async-done | bytes 262160 | tf_op jit(solution)/shard_map/psum | solution.py:54
  260.9 1.4 fusion.26
  262.3 2.9 select_multiply_fusion.1
  265.2 1.7 slice_negate_fusion.1
  266.9 6.8 %fusion.31 = f32[8,64,128]{2,1,0:T(8,128)} fusion(f32[16,8,64,64]{3,2,0,1:T(8,128)S(1)} %get-tuple-element.10, f32[16,8,64,64]{3,2,0,1:T(8,128)S(1)} %get-tuple-element.9, f32[16,8,64,128]{3,2,0,1:T(8,128)S(1)} %select_multiply_fusion.1, f32[1,16,64,128]{3,2,1,0:T(8,128)S(1)} %all-gather.2), kind=kOutput, calls=%fused_computation.41 | convolution fusion | flops 1614807040 | bytes 9175040 | tf_op jit(solution)/shard_map/sik,sckj->cij/dot_general | solution.py:23
  273.7 0.0 all-reduce.8.cloned.1.call-update
  273.7 0.3 all-reduce.10.cloned.1.call-start
  274.0 0.1 slice_negate_fusion.5
  274.2 106.4 %all-reduce.8.cloned.1.call-done = f32[8,64,128]{2,1,0:T(8,128)} async-done(((f32[8,64,128]{2,1,0:T(8,128)}), f32[8,64,128]{2,1,0:T(8,128)}) %all-reduce.8.cloned.1.call-update) | async-done | bytes 262160 | tf_op jit(solution)/shard_map/psum | solution.py:54
  380.6 1.4 fusion.25
  382.0 0.1 slice_negate_fusion.4
  382.1 3.1 select_multiply_fusion
  385.3 1.7 slice_negate_fusion
  386.9 6.8 %fusion.28 = f32[8,64,128]{2,1,0:T(8,128)} fusion(f32[16,8,64,64]{3,2,0,1:T(8,128)S(1)} %get-tuple-element.8, f32[16,8,64,64]{3,2,0,1:T(8,128)S(1)} %get-tuple-element.7, f32[16,8,64,128]{3,2,0,1:T(8,128)S(1)} %select_multiply_fusion, f32[1,16,64,128]{3,2,1,0:T(8,128)S(1)} %all-gather.3), kind=kOutput, calls=%fused_computation.40 | convolution fusion | flops 1614807040 | bytes 9175040 | tf_op jit(solution)/shard_map/sik,sckj->cij/dot_general | solution.py:23
  393.7 0.0 all-reduce.10.cloned.1.call-update
  393.8 0.5 convolution_bitcast_fusion
  394.2 106.4 %all-reduce.10.cloned.1.call-done = f32[8,64,128]{2,1,0:T(8,128)} async-done(((f32[8,64,128]{2,1,0:T(8,128)}), f32[8,64,128]{2,1,0:T(8,128)}) %all-reduce.10.cloned.1.call-update) | async-done | bytes 262160 | tf_op jit(solution)/shard_map/psum | solution.py:54
  500.6 0.8 fusion.68
  501.4 0.6 pad_maximum_fusion
  (9 shorter events, 0.1 us)
Async XLA Ops:
  6.5 134.7 %copy-start = (f32[64,128]{1,0:T(8,128)S(1)}, f32[64,128]{1,0:T(8,128)}, u32[]{:S(2)}) copy-start(f32[64,128]{1,0:T(8,128)} %param.5) | copy-start | bytes 98308
  6.5 133.5 %all-reduce.12.cloned.1.call-start = ((), (), s32[]{:S(2)}) async-start(), calls=%async_computation.3 | async-start | bytes 1048576 | tf_op jit(solution)/shard_map/psum | solution.py:54
  9.2 4.7 copy-start.1
  9.2 4.7 copy-start.2
  28.0 232.8 %all-reduce.6.cloned.1.call-start = ((), (), s32[]{:S(2)}) async-start(), calls=%async_computation | async-start | bytes 524288 | tf_op jit(solution)/shard_map/psum | solution.py:54
  153.9 226.7 %all-reduce.8.cloned.1.call-start = ((), (), s32[]{:S(2)}) async-start(), calls=%async_computation.1 | async-start | bytes 524288 | tf_op jit(solution)/shard_map/psum | solution.py:54
  273.7 226.9 %all-reduce.10.cloned.1.call-start = ((), (), s32[]{:S(2)}) async-start(), calls=%async_computation.2 | async-start | bytes 524288 | tf_op jit(solution)/shard_map/psum | solution.py:54
Sparse Core Ops, SparseCore 0:
  28.1 111.8 all-reduce.11
  154.0 106.8 all-reduce.5
  273.8 106.6 all-reduce.7
  393.9 106.7 all-reduce.9
where the time goes:
time: 509 us
  waiting for transfers between devices  425 us (83%)
  matrix products  35.2 us (7%)
  other arithmetic  25.7 us (5%)
  between operations  13.3 us (3%)
  blocking collectives  9 us (2%)
    psum x4, waiting for transfers between devices, on_device(): memory = lax.psum(partial_value, 'mid')  425 us
    dot_general x4, matrix products, integral(): jnp.einsum('sik,sckj->cij', kernel, stacked, precision=lax.Precision.HIGH...  30.4 us
    mul x4, other arithmetic, integral(): masked = block * keep[:, :, None, None]  11.2 us
    neg x8, other arithmetic, turn_pair(): turned = jnp.concatenate([-block[..., half:], block[..., :half]], axis=-1)  11.2 us
  transfers between devices with their start and end apart: 4, of which 4 were waited for; matrix products, arithmetic and copies ran while one was open for 0% of the time, Pallas kernels for 0%

commit v1 on v0

v1 whole, which is shorter than its diff:
```python
import functools

import jax
import jax.numpy as jnp
from jax import lax
from jax.experimental import pallas as pl
from jax.experimental.pallas import tpu as pltpu
from jax.sharding import PartitionSpec as P

MESH = pl.DeviceIdType.MESH
PLANE = 4
F32 = jnp.float32
BF16 = jnp.bfloat16


def split(value):
    high = value.astype(BF16)
    return high, (value - high.astype(F32)).astype(BF16)


def turn(value):
    half = value.shape[-1] // 2
    rolled = pltpu.roll(value, half, 1)
    lane = lax.broadcasted_iota(jnp.int32, value.shape, 1)
    return jnp.where(lane < half, -rolled, rolled)


def kernel(
    n, f, hist_ref, sigma_ref, prop_ref, out_ref,
    hist, sig, sbuf, lhs, rhs, part, rx1, rx2, rz, stage, outb,
    hist_sem, sig_local, sig_send, sig_recv, s_local, s_send, s_recv,
    sx_send, sx_recv, x1_send, x1_recv, x2_send, x2_recv, z_send, z_recv,
    o_send, o_recv,
):
    m = lax.axis_index("mid")
    q = lax.axis_index("fin")
    slots, cols, rows, lanes = hist_ref.shape
    steps, rf = sigma_ref.shape[0], sigma_ref.shape[2]
    width, ncol = n * slots, f * cols
    planes = n // PLANE
    rc = rows // n
    half = lanes // 2
    depth = slots * half
    x, y, z = m % 2, (m // 2) % 2, m // PLANE
    xy = m % PLANE
    bits = n.bit_length() - 1
    across_x, across_y = m + 1 - 2 * x, m + 2 - 4 * y

    def remote(src, dst, send, recv, **where):
        return pltpu.make_async_remote_copy(
            src_ref=src, dst_ref=dst, send_sem=send, recv_sem=recv,
            device_id=where, device_id_type=MESH,
        )

    def col_time(local, fin):
        return ((fin * cols + local) * width) // ncol

    def owner_plane(g):
        first = (col_time(g * PLANE, q) // slots) // PLANE
        return (first + planes - 1) // 2

    def active(plane, local):
        return (plane * PLANE + PLANE) * slots - 1 >= col_time(local, q)

    near = ((x, 1, y, 2), (y, 2, x, 1))

    def column(g, flip1, flip2):
        b1, w1, b2, w2 = near[g]
        b1 = 1 - b1 if flip1 else b1
        b2 = 1 - b2 if flip2 else b2
        return g * PLANE + b1 * w1 + b2 * w2

    partner = ((across_x, across_y), (across_y, across_x))
    order = []
    for flip1 in (True, False):
        for g in range(2):
            order.append((column(g, flip1, True), column(g, flip1, False)))

    own_sigma = pltpu.make_async_copy(sigma_ref, sig.at[q], sig_local)
    own_sigma.start()

    def s_copies():
        return [
            pltpu.make_async_copy(
                sigma_ref.at[k, pl.ds(0, k)],
                sbuf.at[q, pl.ds(k * (k - 1) // 2, k)],
                s_local.at[k - 1],
            )
            for k in range(1, steps)
        ]

    @pl.when(m == 0)
    def _():
        for copy in s_copies():
            copy.start()

    loads = []
    for i, pair in enumerate(order):
        for j, c in enumerate(pair):
            copy = pltpu.make_async_copy(
                hist_ref.at[:, c], hist.at[c], hist_sem.at[2 * i + j]
            )
            copy.start()
            loads.append(copy)

    barrier = pltpu.get_barrier_semaphore()
    for d in range(1, n):
        pl.semaphore_signal(barrier, inc=1, device_id={"mid": (m + d) % n}, device_id_type=MESH)
    for d in range(1, f):
        pl.semaphore_signal(barrier, inc=1, device_id={"fin": (q + d) % f}, device_id_type=MESH)
    pl.semaphore_wait(barrier, n - 1 + f - 1)

    sig_out = []
    for d in range(1, f):
        copy = remote(sigma_ref, sig.at[q], sig_send.at[d], sig_recv.at[q], fin=(q + d) % f)
        copy.start()
        sig_out.append(copy)

    def s_copy(b):
        return remote(sbuf.at[q], sbuf.at[q], s_send.at[b], s_recv, mid=(m + (1 << b)) % n)

    def broadcast(b):
        if b > 0:
            @pl.when((m >= (1 << (b - 1))) & (m < (1 << b)))
            def _():
                s_copy(b - 1).wait_recv()
        else:
            @pl.when(m == 0)
            def _():
                for copy in s_copies():
                    copy.wait()

        if b < bits:
            @pl.when(m < (1 << b))
            def _():
                s_copy(b).start()

    broadcast(0)

    own_sigma.wait()
    for d in range(1, f):
        src = (q + f - d) % f
        remote(sigma_ref, sig.at[src], sig_send.at[d], sig_recv.at[src], fin=src).wait_recv()
    lane = lax.broadcasted_iota(jnp.int32, (rf, lanes), 1)
    is_last = (m == n - 1).astype(F32)
    for fq in range(f):
        for k in range(steps):
            for t in range(slots // 2):
                a, b = sig[fq, k, 2 * t], sig[fq, k, 2 * t + 1]
                if 2 * t < k:
                    a = a * (m * slots + 2 * t >= k).astype(F32)
                if 2 * t + 1 < k:
                    b = b * (m * slots + 2 * t + 1 >= k).astype(F32)
                if k == 0 and 2 * t + 2 == slots:
                    b = b + prop_ref[fq * rf:(fq + 1) * rf] * is_last
                real = jnp.where(lane < half, a, pltpu.roll(b, half, 1))
                imag = jnp.where(lane < half, pltpu.roll(a, half, 1), b)
                for part_id, value in enumerate((real, imag)):
                    row = (part_id * steps + k) * rows + fq * rf
                    high, low = split(value)
                    lhs[row:row + rf, t * lanes:(t + 1) * lanes] = high
                    lhs[row:row + rf, depth + t * lanes:depth + (t + 1) * lanes] = low

    def compute(i):
        for j, c in enumerate(order[i]):
            loads[2 * i + j].wait()
            start = col_time(c, q)
            for s in range(slots):
                keep = (m * slots + s >= start).astype(F32)
                high, low = split(hist[c, s] * keep)
                rhs[s * half:(s + 1) * half, j * lanes:(j + 1) * lanes] = high
                rhs[depth + s * half:depth + (s + 1) * half, j * lanes:(j + 1) * lanes] = low
        dot = functools.partial(jnp.dot, preferred_element_type=F32)
        total = dot(lhs[:, :depth], rhs[:depth])
        total = total + dot(lhs[:, :depth], rhs[depth:])
        total = total + dot(lhs[:, depth:], rhs[:depth])
        many = steps * rows
        for j, c in enumerate(order[i]):
            block = total[:, j * lanes:(j + 1) * lanes]
            part[c] = block[:many] + turn(block[many:])

    sends = []
    for g in range(2):
        compute(g)
        for j, c in enumerate(order[g]):
            copy = remote(part.at[c], rx1.at[g, j], x1_send.at[g, j], x1_recv.at[g, j], mid=partner[g][0])
            copy.start()
            sends.append(copy)
        broadcast(1 + g)
    first = list(sends)
    second = []
    for g in range(2):
        compute(2 + g)
        c = order[2 + g][0]
        first[2 * g].wait_recv()
        part[c] = part[c] + rx1[g, 0]
        copy = remote(part.at[c], rx2.at[g], x2_send.at[g], x2_recv.at[g], mid=partner[g][1])
        copy.start()
        sends.append(copy)
        second.append(copy)
        if 3 + g <= bits:
            broadcast(3 + g)
    for b in range(5, bits + 1):
        broadcast(b)

    sx_out = []
    for d in range(1, f):
        copy = remote(sbuf.at[q], sbuf.at[q], sx_send.at[d], sx_recv.at[q], fin=(q + d) % f)
        copy.start()
        sx_out.append(copy)

    def z_copy(g, c, src):
        return remote(
            part.at[c], rz.at[g, src], z_send.at[g], z_recv.at[g, src],
            mid=owner_plane(g) * PLANE + xy,
        )

    for g in range(2):
        c = order[2 + g][1]
        first[2 * g + 1].wait_recv()
        second[g].wait_recv()
        part[c] = part[c] + rx1[g, 1] + rx2[g]

        @pl.when((z != owner_plane(g)) & active(z, c))
        def _():
            z_copy(g, c, z).start()

    for d in range(1, f):
        src = (q + f - d) % f
        remote(sbuf.at[src], sbuf.at[src], sx_send.at[d], sx_recv.at[src], fin=src).wait_recv()

    def o_copy(g, d, c):
        to = (m + d) % n
        return remote(stage.at[g, to], outb.at[c], o_send.at[g, d], o_recv.at[c], mid=to)

    for g in range(2):
        c = order[2 + g][1]

        @pl.when(z == owner_plane(g))
        def _():
            for src in range(planes):
                @pl.when((src != z) & active(src, c))
                def _():
                    z_copy(g, c, src).wait_recv()
                    part[c] = part[c] + rz[g, src]

            row = [part[c, k * rows:(k + 1) * rows] for k in range(steps)]
            for j in range(steps):
                for to in range(n):
                    stage[g, to, j] = row[j][to * rc:(to + 1) * rc]
                if j + 1 == steps:
                    break
                blocks = []
                for k in range(j + 1, steps):
                    pieces = [sbuf[fq, k * (k - 1) // 2 + j] for fq in range(f)]
                    weight = jnp.concatenate(pieces, axis=0)
                    blocks.append(weight + prop_ref[...] if k == j + 1 else weight)
                weights = jnp.concatenate(blocks, axis=0)
                stacked = jnp.concatenate([row[j], turn(row[j])], axis=0)
                terms = jnp.dot(
                    weights, stacked, preferred_element_type=F32,
                    precision=lax.Precision.HIGHEST,
                )
                for k in range(j + 1, steps):
                    row[k] = row[k] + terms[(k - j - 1) * rows:(k - j) * rows]
            for d in range(1, n):
                o_copy(g, d, c).start()
            outb[c] = stage[g, m]

    for g in range(2):
        for p in range(PLANE):
            c = g * PLANE + p

            @pl.when(owner_plane(g) * PLANE + p != m)
            def _():
                o_copy(g, 1, c).wait_recv()

    out_ref[...] = outb[...]

    for copy in sig_out + sx_out + sends:
        copy.wait_send()
    for b in range(bits):
        @pl.when(m < (1 << b))
        def _():
            s_copy(b).wait_send()
    for g in range(2):
        c = order[2 + g][1]

        @pl.when((z != owner_plane(g)) & active(z, c))
        def _():
            z_copy(g, c, z).wait_send()

        @pl.when(z == owner_plane(g))
        def _():
            for d in range(1, n):
                o_copy(g, d, c).wait_send()


def solution(mesh):
    n, f = mesh.shape["mid"], mesh.shape["fin"]

    def on_device(history, sigma, propagator):
        slots, cols, rows, lanes = history.shape
        steps, rf = sigma.shape[0], sigma.shape[2]
        rc, depth = rows // n, slots * lanes // 2
        planes, pairs = n // PLANE, steps * (steps - 1) // 2
        many = steps * rows
        bits = n.bit_length() - 1
        dma = pltpu.SemaphoreType.DMA
        anywhere = pl.BlockSpec(memory_space=pl.ANY)
        vmem = pl.BlockSpec(memory_space=pltpu.VMEM)
        out = pl.pallas_call(
            functools.partial(kernel, n, f),
            out_shape=jax.ShapeDtypeStruct((cols, steps, rc, lanes), F32),
            in_specs=[anywhere, anywhere, vmem],
            out_specs=vmem,
            scratch_shapes=[
                pltpu.VMEM((cols, slots, rows, lanes), F32),
                pltpu.VMEM((f, steps, slots, rf, lanes), F32),
                pltpu.VMEM((f, pairs, rf, lanes), F32),
                pltpu.VMEM((2 * many, 2 * depth), BF16),
                pltpu.VMEM((2 * depth, 2 * lanes), BF16),
                pltpu.VMEM((cols, many, lanes), F32),
                pltpu.VMEM((2, 2, many, lanes), F32),
                pltpu.VMEM((2, many, lanes), F32),
                pltpu.VMEM((2, planes, many, lanes), F32),
                pltpu.VMEM((2, n, steps, rc, lanes), F32),
                pltpu.VMEM((cols, steps, rc, lanes), F32),
                dma((cols,)), dma, dma((f,)), dma((f,)),
                dma((steps - 1,)), dma((bits,)), dma,
                dma((f,)), dma((f,)),
                dma((2, 2)), dma((2, 2)), dma((2,)), dma((2,)),
                dma((2,)), dma((2, planes)),
                dma((2, n)), dma((cols,)),
            ],
            compiler_params=pltpu.CompilerParams(
                collective_id=0, has_side_effects=True, vmem_limit_bytes=48 * 2**20
            ),
        )(history, sigma, propagator)
        return jnp.transpose(out, (1, 0, 2, 3))

    in_specs = (P("mid", "fin", None, None), P(None, "mid", "fin", None), P())
    return jax.shard_map(
        on_device, mesh=mesh, in_specs=in_specs, out_specs=P(None, "fin", "mid", None),
        check_vma=False,
    )
```

time: 509 us -> 43.2 us (0.08)
  waiting for transfers between devices: 425 us -> 0 us
  Pallas kernels: 0 us -> 38.2 us
  matrix products: 35.2 us -> 0 us
  other arithmetic: 25.7 us -> 0 us
  between operations: 13.3 us -> 0.01 us
  blocking collectives: 9 us -> 0 us
    psum x4 -> x0, waiting for transfers between devices: 425 us -> none  [on_device(): memory = lax.psum(partial_value, 'mid')]
    pallas_call x0 -> x1, Pallas kernels: none -> 38.2 us  [on_device(): pl.pallas_call(functools.partial(kernel, n, f), out_shape=jax.ShapeDtypeS...]
    dot_general x8 -> x0, matrix products: 35.2 us -> none  [the longest x4 30.4 us: integral(): jnp.einsum('sik,sckj->cij', kernel, stacked, precision=lax.Precision.HIGH...]
    mul x4 -> x0, other arithmetic: 11.2 us -> none  [integral(): masked = block * keep[:, :, None, None]]
    neg x8 -> x0, other arithmetic: 11.2 us -> none  [turn_pair(): turned = jnp.concatenate([-block[..., half:], block[..., :half]], axis=-1)]
    all_gather x4 -> x0, blocking collectives: 9 us -> none  [on_device(): kernel = lax.all_gather(sigma[step], 'fin', axis=1, tiled=True)]
  transfers between devices with their start and end apart: 4 -> 0, of which waited for: 4 -> 0; matrix products, arithmetic and copies ran while one was open for 0% -> 0% of each run, Pallas kernels for 0% -> 0%
where the time goes in v1:
time: 43.2 us; the launch traced here: 43 us
  Pallas kernels  38.2 us (88%)
  local copies, waits for them, and re-layouts  4.81 us (11%)
    pallas_call x1, Pallas kernels, on_device(): pl.pallas_call(functools.partial(kernel, n, f), out_shape=jax.ShapeDtypeS...  38.2 us
    unnamed x6, local copies, waits for them, and re-layouts  4.17 us

profile of v1, /device:TPU:0, one launch (start us, length us, event | category | flops | bytes accessed | tf_op | source)
XLA Modules:
  0.0 43.0 jit_solution(15414087185928513574)
XLA Ops:
  0.0 0.0 copy-start
  0.0 2.2 %copy-done = f32[16,8,64,128]{3,2,1,0:T(8,128)S(1)} copy-done((f32[16,8,64,128]{3,2,1,0:T(8,128)S(1)}, f32[16,8,64,128]{3,2,1,0:T(8,128)}, u32[]{:S(2)}) %copy-start) | copy-done | bytes 4194328
  2.2 0.0 copy-start.1
  2.2 1.2 %copy-done.1 = f32[4,16,32,128]{3,2,1,0:T(8,128)S(1)} copy-done((f32[4,16,32,128]{3,2,1,0:T(8,128)S(1)}, f32[4,16,32,128]{3,2,1,0:T(8,128)}, u32[]{:S(2)}) %copy-start.1) | copy-done | bytes 1048600
  3.4 0.0 copy-start.2
  3.4 0.8 %copy-done.2 = f32[64,128]{1,0:T(8,128)S(1)} copy-done((f32[64,128]{1,0:T(8,128)S(1)}, f32[64,128]{1,0:T(8,128)}, u32[]{:S(2)}) %copy-start.2) | copy-done | bytes 32792
  4.2 38.2 %shard_map.37 = f32[8,4,4,128]{3,2,1,0:T(4,128)S(1)} custom-call(f32[16,8,64,128]{3,2,1,0:T(8,128)S(1)} %copy-done, f32[4,16,32,128]{3,2,1,0:T(8,128)S(1)} %copy-done.1, f32[64,128]{1,0:T(8,128)S(1)} %copy-done.2), custom_call_target="tpu_custom_call" | custom-call | tf_op jit(solution)/shard_map/pallas_call | solution.py:312
  42.4 0.6 %copy.4 = f32[4,8,4,128]{3,2,1,0:T(4,128)} copy(f32[4,8,4,128]{3,2,0,1:T(4,128)S(1)} %bitcast.1) | data formatting | bytes 131072 | tf_op jit(solution)/shard_map/transpose | solution.py:340
Async XLA Ops:
  0.0 2.2 %copy-start = (f32[16,8,64,128]{3,2,1,0:T(8,128)S(1)}, f32[16,8,64,128]{3,2,1,0:T(8,128)}, u32[]{:S(2)}) copy-start(f32[16,8,64,128]{3,2,1,0:T(8,128)} %hist_ref.1) | copy-start | bytes 12582916
  2.2 1.2 %copy-start.1 = (f32[4,16,32,128]{3,2,1,0:T(8,128)S(1)}, f32[4,16,32,128]{3,2,1,0:T(8,128)}, u32[]{:S(2)}) copy-start(f32[4,16,32,128]{3,2,1,0:T(8,128)} %sigma_ref.1) | copy-start | bytes 3145732
  3.4 0.8 %copy-start.2 = (f32[64,128]{1,0:T(8,128)S(1)}, f32[64,128]{1,0:T(8,128)}, u32[]{:S(2)}) copy-start(f32[64,128]{1,0:T(8,128)} %prop_ref.1) | copy-start | bytes 98308

commit v2 on v1

v2 whole, which is shorter than its diff:
```python
import functools

import jax
import jax.numpy as jnp
from jax import lax
from jax.experimental import pallas as pl
from jax.experimental.pallas import tpu as pltpu
from jax.sharding import PartitionSpec as P

MESH = pl.DeviceIdType.MESH
PLANE = 4
F32 = jnp.float32
BF16 = jnp.bfloat16


def split(value):
    high = value.astype(BF16)
    return high, (value - high.astype(F32)).astype(BF16)


def turn(value):
    half = value.shape[-1] // 2
    rolled = pltpu.roll(value, half, 1)
    lane = lax.broadcasted_iota(jnp.int32, value.shape, 1)
    return jnp.where(lane < half, -rolled, rolled)


def kernel(
    n, f, hist_ref, sigma_ref, prop_ref, out_ref,
    hist, sig, sbuf, lhs, rhs, part, rx1, rx2, rz, stage, outb,
    hist_sem, sig_local, sig_send, sig_recv, s_local, s_send, s_recv,
    sx_send, sx_recv, greet, x1_send, x1_recv, x2_send, x2_recv, z_send, z_recv,
    o_send, o_recv,
):
    m = lax.axis_index("mid")
    q = lax.axis_index("fin")
    slots, cols, rows, lanes = hist_ref.shape
    steps, rf = sigma_ref.shape[0], sigma_ref.shape[2]
    width, ncol = n * slots, f * cols
    planes = n // PLANE
    rc = rows // n
    half = lanes // 2
    depth = slots * half
    x, y, z = m % 2, (m // 2) % 2, m // PLANE
    xy = m % PLANE
    bits = n.bit_length() - 1
    across_x, across_y = m + 1 - 2 * x, m + 2 - 4 * y

    def remote(src, dst, send, recv, **where):
        return pltpu.make_async_remote_copy(
            src_ref=src, dst_ref=dst, send_sem=send, recv_sem=recv,
            device_id=where, device_id_type=MESH,
        )

    def col_time(local, fin):
        return ((fin * cols + local) * width) // ncol

    def owner_plane(g):
        first = (col_time(g * PLANE, q) // slots) // PLANE
        return (first + planes - 1) // 2

    def active(plane, g):
        return (plane * PLANE + PLANE) * slots - 1 >= col_time(g * PLANE, q)

    near = ((x, 1, y, 2), (y, 2, x, 1))

    def column(g, flip1, flip2):
        b1, w1, b2, w2 = near[g]
        b1 = 1 - b1 if flip1 else b1
        b2 = 1 - b2 if flip2 else b2
        return g * PLANE + b1 * w1 + b2 * w2

    partner = ((across_x, across_y), (across_y, across_x))
    order = []
    for flip1 in (True, False):
        for g in range(2):
            order.append((column(g, flip1, True), column(g, flip1, False)))

    own_sigma = pltpu.make_async_copy(sigma_ref, sig.at[q], sig_local)
    own_sigma.start()

    def s_copies():
        return [
            pltpu.make_async_copy(
                sigma_ref.at[k, pl.ds(0, k)],
                sbuf.at[q, pl.ds(k * (k - 1) // 2, k)],
                s_local.at[k - 1],
            )
            for k in range(1, steps)
        ]

    @pl.when(m == 0)
    def _():
        for copy in s_copies():
            copy.start()

    loads = []
    for i, pair in enumerate(order):
        for j, c in enumerate(pair):
            copy = pltpu.make_async_copy(
                hist_ref.at[:, c], hist.at[c], hist_sem.at[2 * i + j]
            )
            copy.start()
            loads.append(copy)

    barrier = pltpu.get_barrier_semaphore()
    for to in (across_x, across_y, *((m + PLANE * d) % n for d in range(1, planes))):
        pl.semaphore_signal(barrier, inc=1, device_id={"mid": to}, device_id_type=MESH)
    for d in range(1, f):
        pl.semaphore_signal(barrier, inc=1, device_id={"fin": (q + d) % f}, device_id_type=MESH)

    def build(fq):
        lane = lax.broadcasted_iota(jnp.int32, (rf, lanes), 1)
        is_last = (m == n - 1).astype(F32)
        for k in range(steps):
            for t in range(slots // 2):
                a, b = sig[fq, k, 2 * t], sig[fq, k, 2 * t + 1]
                if 2 * t < k:
                    a = a * (m * slots + 2 * t >= k).astype(F32)
                if 2 * t + 1 < k:
                    b = b * (m * slots + 2 * t + 1 >= k).astype(F32)
                if k == 0 and 2 * t + 2 == slots:
                    b = b + prop_ref[pl.ds(pl.multiple_of(fq * rf, rf), rf)] * is_last
                real = jnp.where(lane < half, a, pltpu.roll(b, half, 1))
                imag = jnp.where(lane < half, pltpu.roll(a, half, 1), b)
                for part_id, value in enumerate((real, imag)):
                    row = (part_id * steps + k) * rf
                    high, low = split(value)
                    lhs[fq, row:row + rf, t * lanes:(t + 1) * lanes] = high
                    lhs[fq, row:row + rf, depth + t * lanes:depth + (t + 1) * lanes] = low

    own_sigma.wait()
    build(q)
    pl.semaphore_wait(barrier, 2 + planes - 1 + f - 1)

    sig_out = []
    for d in range(1, f):
        copy = remote(sigma_ref, sig.at[q], sig_send.at[d], sig_recv.at[q], fin=(q + d) % f)
        copy.start()
        sig_out.append(copy)
    pl.semaphore_signal(greet.at[0], inc=1, device_id={"mid": across_x}, device_id_type=MESH)

    route = [0, 1, *reversed(range(2, bits))]

    def only(known):
        rest = 0
        for b in range(bits):
            if b not in known:
                rest = rest + (m // (1 << b)) % 2
        return rest == 0

    def s_copy(i):
        b = route[i]
        return remote(sbuf.at[q], sbuf.at[q], s_send.at[b], s_recv, mid=(m + (1 << b)) % n)

    def broadcast(i):
        if i > 0:
            @pl.when(only(route[:i]) & ((m // (1 << route[i - 1])) % 2 == 1))
            def _():
                s_copy(i - 1).wait_recv()
        else:
            @pl.when(m == 0)
            def _():
                for copy in s_copies():
                    copy.wait()

        if i < bits:
            @pl.when(only(route[:i]))
            def _():
                s_copy(i).start()

    broadcast(0)

    def prepare(i):
        for j, c in enumerate(order[i]):
            loads[2 * i + j].wait()

        @pl.when(active(z, i % 2))
        def _():
            for j, c in enumerate(order[i]):
                start = col_time(c, q)
                for s in range(slots):
                    keep = (m * slots + s >= start).astype(F32)
                    high, low = split(hist[c, s] * keep)
                    rhs[i, s * half:(s + 1) * half, j * lanes:(j + 1) * lanes] = high
                    rhs[i, depth + s * half:depth + (s + 1) * half, j * lanes:(j + 1) * lanes] = low

    def compute(i, fq):
        dot = functools.partial(jnp.dot, preferred_element_type=F32)
        total = dot(lhs[fq, :, :depth], rhs[i, :depth])
        total = total + dot(lhs[fq, :, :depth], rhs[i, depth:])
        total = total + dot(lhs[fq, :, depth:], rhs[i, :depth])
        many = steps * rf
        for j, c in enumerate(order[i]):
            block = total[:, j * lanes:(j + 1) * lanes]
            part[c, fq] = block[:many] + turn(block[many:])

    def x1_copy(g, j, fq):
        return remote(
            part.at[order[g][j], fq], rx1.at[g, j, fq],
            x1_send.at[g, j, fq], x1_recv.at[g, j, fq], mid=partner[g][0],
        )

    def x2_copy(g, fq):
        return remote(
            part.at[order[2 + g][0], fq], rx2.at[g, fq],
            x2_send.at[g, fq], x2_recv.at[g, fq], mid=partner[g][1],
        )

    def z_copy(g, fq, src):
        return remote(
            part.at[order[2 + g][1], fq], rz.at[g, src, fq],
            z_send.at[g, fq], z_recv.at[g, src, fq], mid=owner_plane(g) * PLANE + xy,
        )

    def send(g, fq):
        @pl.when(active(z, g))
        def _():
            compute(g, fq)
            for j in range(2):
                x1_copy(g, j, fq).start()

    def hold(g, fq):
        @pl.when(active(z, g))
        def _():
            compute(2 + g, fq)

    def forward(g, fq):
        @pl.when(active(z, g))
        def _():
            c = order[2 + g][0]
            x1_copy(g, 0, fq).wait_recv()
            part[c, fq] = part[c, fq] + rx1[g, 0, fq]
            x2_copy(g, fq).start()

    def finish(g, fq):
        @pl.when(active(z, g))
        def _():
            c = order[2 + g][1]
            x1_copy(g, 1, fq).wait_recv()
            x2_copy(g, fq).wait_recv()
            part[c, fq] = part[c, fq] + rx1[g, 1, fq] + rx2[g, fq]

            @pl.when(z != owner_plane(g))
            def _():
                z_copy(g, fq, z).start()

    for g in range(2):
        prepare(g)
        send(g, q)
    for g in range(2):
        prepare(2 + g)
        hold(g, q)
    broadcast(1)
    pl.semaphore_wait(greet.at[0], 1)
    pl.semaphore_signal(greet.at[1], inc=1, device_id={"mid": across_y}, device_id_type=MESH)
    others = [(q + r) % f for r in range(1, f)]
    for r, fq in enumerate(others):
        remote(sigma_ref, sig.at[fq], sig_send.at[1 + r], sig_recv.at[fq], fin=fq).wait_recv()
        build(fq)
        for g in range(2):
            send(g, fq)
    broadcast(2)
    for g in range(2):
        forward(g, q)
    for fq in others:
        for g in range(2):
            hold(g, fq)
    if bits >= 3:
        broadcast(3)
    for fq in others:
        for g in range(2):
            forward(g, fq)
    for g in range(2):
        finish(g, q)
    for i in range(4, bits + 1):
        broadcast(i)

    sx_out = []
    for d in range(1, f):
        copy = remote(sbuf.at[q], sbuf.at[q], sx_send.at[d], sx_recv.at[q], fin=(q + d) % f)
        copy.start()
        sx_out.append(copy)
    for fq in others:
        for g in range(2):
            finish(g, fq)
    pl.semaphore_wait(greet.at[1], 1)

    for fq in others:
        remote(sbuf.at[fq], sbuf.at[fq], sx_send.at[0], sx_recv.at[fq], fin=fq).wait_recv()

    def o_copy(g, d, c):
        to = (m + d) % n
        return remote(stage.at[g, to], outb.at[c], o_send.at[g, d], o_recv.at[c], mid=to)

    for g in range(2):
        c = order[2 + g][1]

        @pl.when(z == owner_plane(g))
        def _():
            for src in range(planes):
                @pl.when((src != z) & active(src, g))
                def _():
                    for fq in range(f):
                        z_copy(g, fq, src).wait_recv()
                    part[c] = part[c] + rz[g, src]

            row = []
            for k in range(steps):
                pieces = [part[c, fq, k * rf:(k + 1) * rf] for fq in range(f)]
                row.append(jnp.concatenate(pieces, axis=0))
            for j in range(steps):
                for to in range(n):
                    stage[g, to, j] = row[j][to * rc:(to + 1) * rc]
                if j + 1 == steps:
                    break
                blocks = []
                for k in range(j + 1, steps):
                    pieces = [sbuf[fq, k * (k - 1) // 2 + j] for fq in range(f)]
                    weight = jnp.concatenate(pieces, axis=0)
                    blocks.append(weight + prop_ref[...] if k == j + 1 else weight)
                weights = jnp.concatenate(blocks, axis=0)
                stacked = jnp.concatenate([row[j], turn(row[j])], axis=0)
                terms = jnp.dot(
                    weights, stacked, preferred_element_type=F32,
                    precision=lax.Precision.HIGHEST,
                )
                for k in range(j + 1, steps):
                    row[k] = row[k] + terms[(k - j - 1) * rows:(k - j) * rows]
            for d in range(1, n):
                o_copy(g, d, c).start()
            outb[c] = stage[g, m]

    for g in range(2):
        for p in range(PLANE):
            c = g * PLANE + p

            @pl.when(owner_plane(g) * PLANE + p != m)
            def _():
                o_copy(g, 1, c).wait_recv()

    out_ref[...] = outb[...]

    for copy in sig_out + sx_out:
        copy.wait_send()
    for i in range(bits):
        @pl.when(only(route[:i]))
        def _():
            s_copy(i).wait_send()
    for g in range(2):
        c = order[2 + g][1]

        @pl.when(active(z, g))
        def _():
            for fq in range(f):
                x1_copy(g, 0, fq).wait_send()
                x1_copy(g, 1, fq).wait_send()
                x2_copy(g, fq).wait_send()

            @pl.when(z != owner_plane(g))
            def _():
                for fq in range(f):
                    z_copy(g, fq, z).wait_send()

        @pl.when(z == owner_plane(g))
        def _():
            for d in range(1, n):
                o_copy(g, d, c).wait_send()


def solution(mesh):
    n, f = mesh.shape["mid"], mesh.shape["fin"]

    def on_device(history, sigma, propagator):
        slots, cols, rows, lanes = history.shape
        steps, rf = sigma.shape[0], sigma.shape[2]
        rc, depth = rows // n, slots * lanes // 2
        planes, pairs = n // PLANE, steps * (steps - 1) // 2
        many = steps * rf
        bits = n.bit_length() - 1
        dma = pltpu.SemaphoreType.DMA
        anywhere = pl.BlockSpec(memory_space=pl.ANY)
        vmem = pl.BlockSpec(memory_space=pltpu.VMEM)
        out = pl.pallas_call(
            functools.partial(kernel, n, f),
            out_shape=jax.ShapeDtypeStruct((cols, steps, rc, lanes), F32),
            in_specs=[anywhere, anywhere, vmem],
            out_specs=vmem,
            scratch_shapes=[
                pltpu.VMEM((cols, slots, rows, lanes), F32),
                pltpu.VMEM((f, steps, slots, rf, lanes), F32),
                pltpu.VMEM((f, pairs, rf, lanes), F32),
                pltpu.VMEM((f, 2 * many, 2 * depth), BF16),
                pltpu.VMEM((4, 2 * depth, 2 * lanes), BF16),
                pltpu.VMEM((cols, f, many, lanes), F32),
                pltpu.VMEM((2, 2, f, many, lanes), F32),
                pltpu.VMEM((2, f, many, lanes), F32),
                pltpu.VMEM((2, planes, f, many, lanes), F32),
                pltpu.VMEM((2, n, steps, rc, lanes), F32),
                pltpu.VMEM((cols, steps, rc, lanes), F32),
                dma((cols,)), dma, dma((f,)), dma((f,)),
                dma((steps - 1,)), dma((bits,)), dma,
                dma((f,)), dma((f,)), pltpu.SemaphoreType.REGULAR((2,)),
                dma((2, 2, f)), dma((2, 2, f)), dma((2, f)), dma((2, f)),
                dma((2, f)), dma((2, planes, f)),
                dma((2, n)), dma((cols,)),
            ],
            compiler_params=pltpu.CompilerParams(
                collective_id=0, has_side_effects=True, vmem_limit_bytes=60 * 2**20
            ),
        )(history, sigma, propagator)
        return jnp.transpose(out, (1, 0, 2, 3))

    in_specs = (P("mid", "fin", None, None), P(None, "mid", "fin", None), P())
    return jax.shard_map(
        on_device, mesh=mesh, in_specs=in_specs, out_specs=P(None, "fin", "mid", None),
        check_vma=False,
    )
```

time: 43.2 us -> 33.4 us (0.77)
  Pallas kernels: 38.2 us -> 31.7 us
  local copies, waits for them, and re-layouts: 4.81 us -> 1.48 us
    pallas_call x1, Pallas kernels: 38.2 us -> 31.7 us  [on_device(): pl.pallas_call(functools.partial(kernel, n, f), out_shape=jax.ShapeDtypeS...]
    unnamed x6 -> x0, local copies, waits for them, and re-layouts: 4.17 us -> none
    transpose x1, local copies, waits for them, and re-layouts: 0.64 us -> 1.48 us  [on_device(): return jnp.transpose(out, (1, 0, 2, 3))]
where the time goes in v2:
time: 33.4 us; the launch traced here: 33.2 us
  Pallas kernels  31.7 us (95%)
  local copies, waits for them, and re-layouts  1.48 us (4%)
    pallas_call x1, Pallas kernels, on_device(): pl.pallas_call(functools.partial(kernel, n, f), out_shape=jax.ShapeDtypeS...  31.7 us
    transpose x1, local copies, waits for them, and re-layouts, on_device(): return jnp.transpose(out, (1, 0, 2, 3))  1.48 us

profile of v2, /device:TPU:0, one launch (start us, length us, event | category | flops | bytes accessed | tf_op | source)
XLA Modules:
  0.0 33.2 jit_solution(11790873804854053006)
XLA Ops:
  0.0 31.7 %shard_map.37 = f32[8,4,4,128]{3,2,1,0:T(4,128)} custom-call(f32[16,8,64,128]{3,2,1,0:T(8,128)} %hist_ref.1, f32[4,16,32,128]{3,2,1,0:T(8,128)} %sigma_ref.1, f32[64,128]{1,0:T(8,128)} %prop_ref.1), custom_call_target="tpu_custom_call" | custom-call | tf_op jit(solution)/shard_map/pallas_call | solution.py:384
  31.7 1.5 %copy.4 = f32[4,8,4,128]{3,2,1,0:T(4,128)} copy(f32[4,8,4,128]{3,2,0,1:T(4,128)} %bitcast.1) | data formatting | bytes 131072 | tf_op jit(solution)/shard_map/transpose | solution.py:412

commit v3 on v2

--- a/solution.py
+++ b/solution.py
@@ -26,9 +26,9 @@
 
 
 def kernel(
-    n, f, hist_ref, sigma_ref, prop_ref, out_ref,
-    hist, sig, sbuf, lhs, rhs, part, rx1, rx2, rz, stage, outb,
-    hist_sem, sig_local, sig_send, sig_recv, s_local, s_send, s_recv,
+    n, f, hist_ref, sigma_ref, prop_hbm, outb,
+    hist, sig, prop_ref, sbuf, lhs, rhs, part, rx1, rx2, rz, stage,
+    hist_sem, prop_sem, sig_local, sig_send, sig_recv, s_local, s_send, s_recv,
     sx_send, sx_recv, greet, x1_send, x1_recv, x2_send, x2_recv, z_send, z_recv,
     o_send, o_recv,
 ):
@@ -78,6 +78,8 @@
 
     own_sigma = pltpu.make_async_copy(sigma_ref, sig.at[q], sig_local)
     own_sigma.start()
+    own_prop = pltpu.make_async_copy(prop_hbm, prop_ref, prop_sem)
+    own_prop.start()
 
     def s_copies():
         return [
@@ -130,6 +132,7 @@
                     lhs[fq, row:row + rf, depth + t * lanes:depth + (t + 1) * lanes] = low
 
     own_sigma.wait()
+    own_prop.wait()
     build(q)
     pl.semaphore_wait(barrier, 2 + planes - 1 + f - 1)
 
@@ -329,7 +332,9 @@
                     row[k] = row[k] + terms[(k - j - 1) * rows:(k - j) * rows]
             for d in range(1, n):
                 o_copy(g, d, c).start()
-            outb[c] = stage[g, m]
+            own = pltpu.make_async_copy(stage.at[g, m], outb.at[c], o_send.at[g, 0])
+            own.start()
+            own.wait()
 
     for g in range(2):
         for p in range(PLANE):
@@ -338,8 +343,6 @@
             @pl.when(owner_plane(g) * PLANE + p != m)
             def _():
                 o_copy(g, 1, c).wait_recv()
-
-    out_ref[...] = outb[...]
 
     for copy in sig_out + sx_out:
         copy.wait_send()
@@ -380,15 +383,15 @@
         bits = n.bit_length() - 1
         dma = pltpu.SemaphoreType.DMA
         anywhere = pl.BlockSpec(memory_space=pl.ANY)
-        vmem = pl.BlockSpec(memory_space=pltpu.VMEM)
         out = pl.pallas_call(
             functools.partial(kernel, n, f),
             out_shape=jax.ShapeDtypeStruct((cols, steps, rc, lanes), F32),
-            in_specs=[anywhere, anywhere, vmem],
-            out_specs=vmem,
+            in_specs=[anywhere, anywhere, anywhere],
+            out_specs=anywhere,
             scratch_shapes=[
                 pltpu.VMEM((cols, slots, rows, lanes), F32),
                 pltpu.VMEM((f, steps, slots, rf, lanes), F32),
+                pltpu.VMEM((rows, lanes), F32),
                 pltpu.VMEM((f, pairs, rf, lanes), F32),
                 pltpu.VMEM((f, 2 * many, 2 * depth), BF16),
                 pltpu.VMEM((4, 2 * depth, 2 * lanes), BF16),
@@ -397,8 +400,7 @@
                 pltpu.VMEM((2, f, many, lanes), F32),
                 pltpu.VMEM((2, planes, f, many, lanes), F32),
                 pltpu.VMEM((2, n, steps, rc, lanes), F32),
-                pltpu.VMEM((cols, steps, rc, lanes), F32),
-                dma((cols,)), dma, dma((f,)), dma((f,)),
+                dma((cols,)), dma, dma, dma((f,)), dma((f,)),
                 dma((steps - 1,)), dma((bits,)), dma,
                 dma((f,)), dma((f,)), pltpu.SemaphoreType.REGULAR((2,)),
                 dma((2, 2, f)), dma((2, 2, f)), dma((2, f)), dma((2, f)),

time: 33.4 us -> 32.1 us (0.961)
  Pallas kernels: 31.7 us -> 30.4 us
    pallas_call x1, Pallas kernels: 31.7 us -> 30.4 us  [on_device(): pl.pallas_call(functools.partial(kernel, n, f), out_shape=jax.ShapeDtypeS...]
where the time goes in v3:
time: 32.1 us; the launch traced here: 31.9 us
  Pallas kernels  30.4 us (95%)
  local copies, waits for them, and re-layouts  1.48 us (5%)
    pallas_call x1, Pallas kernels, on_device(): pl.pallas_call(functools.partial(kernel, n, f), out_shape=jax.ShapeDtypeS...  30.4 us
    transpose x1, local copies, waits for them, and re-layouts, on_device(): return jnp.transpose(out, (1, 0, 2, 3))  1.48 us

profile of v3, /device:TPU:0, one launch (start us, length us, event | category | flops | bytes accessed | tf_op | source)
XLA Modules:
  0.0 31.9 jit_solution(7613119648781670719)
XLA Ops:
  0.0 30.4 %shard_map.37 = f32[8,4,4,128]{3,2,1,0:T(4,128)} custom-call(f32[16,8,64,128]{3,2,1,0:T(8,128)} %hist_ref.1, f32[4,16,32,128]{3,2,1,0:T(8,128)} %sigma_ref.1, f32[64,128]{1,0:T(8,128)} %prop_hbm.1), custom_call_target="tpu_custom_call" | custom-call | tf_op jit(solution)/shard_map/pallas_call | solution.py:386
  30.4 1.5 %copy.4 = f32[4,8,4,128]{3,2,1,0:T(4,128)} copy(f32[4,8,4,128]{3,2,0,1:T(4,128)} %bitcast.1) | data formatting | bytes 131072 | tf_op jit(solution)/shard_map/transpose | solution.py:414
